TPU v7x, 32 devices: a whole 2x2x4 slice. The times are simulated.
32 devices in a mesh: win: 4 (over x, core), src: 8 (over z, y).
Axes of the slice: x: 2, y: 2, z: 4, core: 2. Of those that a mesh axis runs over, the one named last changes fastest.
Arguments:
- strain: bfloat16 [6144, 10240], P('win', 'src'), may hold values from -1000 to 1000
- dead_mask: int32 [4, 10240], P('win', 'src'), may hold values 0 or 1
- src_index: int32 [256], replicated, may hold values from 0 to 10239
Outputs:
- correlations: float32 [4, 256, 32, 10240], P('win', 'src')
All inputs are finite; a program needn't handle non-finite values. No bound on the sum of `dead_mask` on one device may be relied on, other than what follows from the above.
Results may differ from a plain program's by a relative error of at most 0.0041.
Values may be sent and summed in bfloat16 or wider, within the bound.
No kernel may reach another device: no remote copies, remote signals or barrier semaphores. Data moves between devices by JAX's collectives and lax.ppermute only.
A program may use at most 192 MiB of HBM per device.

v0:
```python
import functools
import math

import jax
import jax.numpy as jnp
from jax import lax
from jax.experimental import pallas as pl
from jax.experimental.pallas import tpu as pltpu
from jax.sharding import PartitionSpec as P


LAGS = 32
HALF = 32
EPSILON = 1e-05
TILE = 192
SPAN = 2 * HALF
ROWS = 512
WIDTHS = (512, 512, 256)
FLAT_SENT = 1
VMEM_BYTES = 24 << 20
LAG = (4, 4, 3, 1)


def passed_along(array, axis, by):
    devices = lax.axis_size(axis)
    pairs = [(i, i + by) for i in range(devices) if 0 <= i + by < devices]
    return lax.ppermute(array, axis, pairs)


def normalize_kernel(strain_ref, mask_ref, lead_ref, trail_ref, flat_ref, rows):
    samples = strain_ref.shape[0]
    width = strain_ref.shape[1]
    alive = jnp.broadcast_to(mask_ref[...] > 0, (samples, width))
    rows[:HALF] = lead_ref[...]
    rows[HALF : HALF + samples] = jnp.where(
        alive, strain_ref[...].astype(jnp.float32), 0.0
    ).astype(jnp.bfloat16)
    rows[HALF + samples :] = trail_ref[...]
    out_rows = flat_ref.shape[0]
    row = lax.broadcasted_iota(jnp.int32, (TILE, TILE + SPAN), 0)
    col = lax.broadcasted_iota(jnp.int32, (TILE, TILE + SPAN), 1)
    band = jnp.where((col >= row) & (col <= row + SPAN), 1.0, 0.0).astype(jnp.bfloat16)
    for start in range(0, out_rows, TILE):
        count = min(TILE, out_rows - start)
        near = rows[start : start + count + SPAN]
        sums = jnp.dot(
            band[:count, : count + SPAN], jnp.abs(near), preferred_element_type=jnp.float32
        )
        center = rows[start + HALF : start + HALF + count].astype(jnp.float32)
        flat_ref[start : start + count] = (
            center / (sums / (2 * HALF + 1) + EPSILON)
        ).astype(jnp.bfloat16)


def params():
    return pltpu.CompilerParams(vmem_limit_bytes=VMEM_BYTES)


def normalize_chunk(strain, mask, lead, trail, offset, width):
    samples = strain.shape[0]

    def block(rows):
        return pl.BlockSpec((pl.Element(rows), pl.Element(width)), lambda i: (0, offset))

    return pl.pallas_call(
        normalize_kernel,
        out_shape=jax.ShapeDtypeStruct((samples + HALF, width), jnp.bfloat16),
        grid=(1,),
        in_specs=[block(samples), block(1), block(HALF), block(SPAN)],
        out_specs=pl.BlockSpec((samples + HALF, width), lambda i: (0, 0)),
        scratch_shapes=[pltpu.VMEM((samples + HALF + SPAN, width), jnp.bfloat16)],
        compiler_params=params(),
        cost_estimate=pl.CostEstimate(
            flops=2 * (samples + HALF) * (TILE + SPAN) * width,
            bytes_accessed=4 * samples * width,
            transcendentals=0,
        ),
        name="normalize",
    )(strain, mask, lead, trail)


def select_kernel(index_ref, *refs):
    flats, out_ref = refs[:-1], refs[-1]
    total = jnp.zeros(out_ref.shape, jnp.float32)
    offset = 0
    for flat_ref in flats:
        width = flat_ref.shape[1]
        channel = lax.broadcasted_iota(jnp.int32, (index_ref.shape[0], width), 1) + offset
        onehot = jnp.where(index_ref[...] == channel, 1.0, 0.0).astype(jnp.bfloat16)
        total += lax.dot_general(
            onehot, flat_ref[...], (((1,), (1,)), ((), ())), preferred_element_type=jnp.float32
        )
        offset += width
    out_ref[...] = total.astype(jnp.bfloat16)


def select_sources(flats, index, samples):
    sources = index.shape[0]
    channels = sum(f.shape[1] for f in flats)
    return pl.pallas_call(
        select_kernel,
        out_shape=jax.ShapeDtypeStruct((sources, samples), jnp.bfloat16),
        grid=(samples // 256,),
        in_specs=[pl.BlockSpec((sources, 1), lambda i: (0, 0))]
        + [pl.BlockSpec((256, f.shape[1]), lambda i: (i, 0)) for f in flats],
        out_specs=pl.BlockSpec((sources, 256), lambda i: (0, i)),
        compiler_params=params(),
        cost_estimate=pl.CostEstimate(
            flops=2 * sources * samples * channels,
            bytes_accessed=2 * samples * channels,
            transcendentals=0,
        ),
        name="select",
    )(index[:, None], *flats)


def hankel_kernel(trace_ref, out_ref):
    width = out_ref.shape[1]
    for source in range(trace_ref.shape[0]):
        spread = jnp.broadcast_to(trace_ref[source : source + 1], (LAGS, width))
        shifted = pltpu.roll(spread, 0, 1, stride=1, stride_axis=0)
        out_ref[source * LAGS : (source + 1) * LAGS] = shifted.astype(jnp.bfloat16)


def hankel(traces):
    sources, samples = traces.shape
    width = samples + 128
    padded = jnp.pad(traces.astype(jnp.float32), ((0, 0), (0, 128)))
    return pl.pallas_call(
        hankel_kernel,
        out_shape=jax.ShapeDtypeStruct((sources * LAGS, width), jnp.bfloat16),
        grid=(sources // 8,),
        in_specs=[pl.BlockSpec((8, width), lambda i: (i, 0))],
        out_specs=pl.BlockSpec((8 * LAGS, width), lambda i: (i, 0)),
        compiler_params=params(),
        cost_estimate=pl.CostEstimate(
            flops=sources * LAGS * width, bytes_accessed=2 * sources * LAGS * width, transcendentals=0
        ),
        name="hankel",
    )(padded)


def at_end(spot):
    return (spot == 0) | (spot == 3)


def origin(slot, me):
    spot, side = me >> 1, me & 1
    near = spot < 2
    there = [
        spot,
        spot ^ 1,
        jnp.where(near, 2, 1),
        jnp.where(near, 3, 0),
    ][slot]
    return 2 * there + side


def correlate_kernel(rows, two, aliased, scale, me_ref, *refs):
    refs = list(refs)
    hankels = [refs.pop(0) for _ in range(rows)]
    first = refs.pop(0)
    second = refs.pop(0) if two else None
    if aliased:
        refs.pop(0)
    held = refs.pop()
    out_ref = refs.pop(0)
    depth, width = first.shape
    step = pl.program_id(0)
    each = hankels[0].shape[0] // ROWS

    @pl.when(step == 0)
    def _():
        held[depth:] = jnp.zeros((held.shape[0] - depth, width), held.dtype)
        if two:
            end = at_end(me_ref[0] >> 1)

            @pl.when(end)
            def _():
                held[:depth] = first[...]

            @pl.when(jnp.logical_not(end))
            def _():
                held[:depth] = second[...]
        else:
            held[:depth] = first[...]

    def product(ref, at):
        lagged = ref[pl.ds(pl.multiple_of(at * ROWS, ROWS), ROWS), :]
        return jnp.dot(lagged, held[...], preferred_element_type=jnp.float32) * scale

    if rows == 1:
        out_ref[...] = product(hankels[0], step).reshape(out_ref.shape)
        return
    sent_ref = refs.pop(0)

    @pl.when(step < each)
    def _():
        sent_ref[...] = product(hankels[1], step).reshape(sent_ref.shape).astype(sent_ref.dtype)

    @pl.when(step >= each)
    def _():
        out_ref[...] = product(hankels[0], step - each).reshape(out_ref.shape)


def correlate(hankels, operands, me, place, scale, out, channels):
    lanes, span = hankels[0].shape
    sources = lanes // LAGS
    depth, width = operands[0].shape
    group = ROWS // LAGS
    each = lanes // ROWS
    rows = len(hankels)
    skip = (rows - 1) * each
    resident = pl.BlockSpec(memory_space=pltpu.VMEM)
    in_specs = [resident] * rows
    in_specs += [pl.BlockSpec((depth, width), lambda i, me: (0, 0))] * len(operands)
    arguments = [*hankels, *operands]
    aliases = {}
    if out is not None:
        in_specs.append(pl.BlockSpec(memory_space=pl.ANY))
        arguments.append(out)
        aliases = {len(arguments): 0}
    out_shape = [jax.ShapeDtypeStruct((1, sources, LAGS, channels), jnp.float32)]
    out_specs = [
        pl.BlockSpec(
            (pl.Element(1), pl.Element(group), pl.Element(LAGS), pl.Element(width)),
            lambda i, me: (
                0,
                jnp.maximum(i - skip, 0) * group,
                0,
                pl.multiple_of(place(me[0]), 128),
            ),
        )
    ]
    if rows == 2:
        out_shape.append(jax.ShapeDtypeStruct((sources, LAGS, width), jnp.bfloat16))
        out_specs.append(
            pl.BlockSpec((group, LAGS, width), lambda i, me: (jnp.minimum(i, each - 1), 0, 0))
        )
    return pl.pallas_call(
        functools.partial(correlate_kernel, rows, len(operands) == 2, bool(aliases), scale),
        out_shape=out_shape,
        grid_spec=pltpu.PrefetchScalarGridSpec(
            num_scalar_prefetch=1,
            grid=(rows * each,),
            in_specs=in_specs,
            out_specs=out_specs,
            scratch_shapes=[pltpu.VMEM((span, width), jnp.bfloat16)],
        ),
        input_output_aliases=aliases,
        compiler_params=params(),
        cost_estimate=pl.CostEstimate(
            flops=2 * rows * lanes * span * width,
            bytes_accessed=2 * depth * width + 4 * lanes * width,
            transcendentals=0,
        ),
        name="correlate",
    )(me, *arguments)


def store_kernel(me_ref, got_ref, kept_ref, out_ref):
    out_ref[...] = got_ref[...].astype(jnp.float32)[None]


def store(got, me, place, out):
    sources, lags, width = got.shape
    group = ROWS // LAGS
    return pl.pallas_call(
        store_kernel,
        out_shape=jax.ShapeDtypeStruct(out.shape, out.dtype),
        grid_spec=pltpu.PrefetchScalarGridSpec(
            num_scalar_prefetch=1,
            grid=(sources // group,),
            in_specs=[
                pl.BlockSpec((group, lags, width), lambda i, me: (i, 0, 0)),
                pl.BlockSpec(memory_space=pl.ANY),
            ],
            out_specs=pl.BlockSpec(
                (pl.Element(1), pl.Element(group), pl.Element(lags), pl.Element(width)),
                lambda i, me: (0, i * group, 0, pl.multiple_of(place(me[0]), 128)),
            ),
        ),
        input_output_aliases={2: 0},
        compiler_params=params(),
        cost_estimate=pl.CostEstimate(
            flops=0, bytes_accessed=6 * sources * lags * width, transcendentals=0
        ),
        name="store",
    )(me, got, out)


def hop(array, pairs):
    return lax.ppermute(array, "src", pairs)


def line_of_four(strain, dead_mask, src_index):
    samples, channels = strain.shape
    devices = lax.axis_size("src")
    line = devices // 2
    count = len(WIDTHS)
    offsets = [sum(WIDTHS[:c]) for c in range(count)]
    total = channels * devices
    own = src_index.shape[0] // devices
    scale = 1.0 / math.sqrt(samples)
    me = lax.axis_index("src")
    spot, side = me >> 1, me & 1

    def along(pairs):
        return [(2 * a + s, 2 * b + s) for a, b in pairs for s in range(2)]

    outer = along([(0, 1), (1, 0), (2, 3), (3, 2)])
    inner = along([(1, 2), (2, 1)])
    outward = along([(1, 0), (2, 3)])
    across = [(i, i ^ 1) for i in range(devices)]

    def masked(rows):
        return jnp.where(dead_mask > 0, rows, jnp.zeros((), rows.dtype))

    lead = passed_along(masked(strain[samples - HALF :]), "win", 1)
    trail = passed_along(masked(strain[:SPAN]), "win", -1)
    flats = []
    for c in range(count):
        flats.append(
            normalize_chunk(strain, dead_mask, lead, trail, offsets[c], WIDTHS[c])
        )

    selected = select_sources(flats, src_index - me * channels, samples)
    grouped = selected.reshape(line, 2, own, samples)
    theirs = lax.dynamic_index_in_dim(grouped, 1 - side, 1, keepdims=False)
    mine = lax.dynamic_index_in_dim(grouped, side, 1, keepdims=False)
    mine = mine + hop(theirs, across)
    traces = lax.dynamic_index_in_dim(mine, spot, 0, keepdims=False)
    for by in range(1, line):
        there = lax.dynamic_index_in_dim(mine, (spot + by) & (line - 1), 0, keepdims=False)
        traces = traces + hop(there, along([(i, (i + by) % line) for i in range(line)]))
    partner_traces = hop(traces, across)
    own_rows = hankel(traces)
    partner_rows = hankel(partner_traces)

    def hops(arrays, pairs):
        return [hop(a, pairs) for a in arrays]

    first_out = hops(flats, outer)
    first_in = hops(flats, inner)
    swapped = hops(flats[:FLAT_SENT], across)
    second_out = hops(first_in, outward)
    second_in = hops(first_out, inner)
    third_out = hops(second_in, outward)

    arrivals = [
        [[f] for f in flats],
        [[f] for f in first_out],
        [list(pair) for pair in zip(second_out, first_in)],
        [list(pair) for pair in zip(third_out, second_in)],
    ]
    here = jnp.reshape(me, (1,)).astype(jnp.int32)
    out = None
    waiting = []

    def place(slot, c, partner):
        return lambda me: (origin(slot, me) ^ partner) * channels + offsets[c]

    for slot in range(line):
        for c in range(count):
            if slot == 0 and c < FLAT_SENT:
                for partner, chunk in ((0, flats[c]), (1, swapped[c])):
                    (out,) = correlate(
                        [own_rows], [chunk], here, place(slot, c, partner), scale, out, total
                    )
                continue
            out, made = correlate(
                [own_rows, partner_rows],
                arrivals[slot][c],
                here,
                place(slot, c, 0),
                scale,
                out,
                total,
            )
            waiting.append((hop(made, across), here, place(slot, c, 1)))
            while len(waiting) > LAG[slot]:
                out = store(*waiting.pop(0), out)
    while waiting:
        out = store(*waiting.pop(0), out)
    return out


def gathered(strain, dead_mask, src_index):
    samples, channels = strain.shape
    devices = lax.axis_size("src")
    scale = 1.0 / math.sqrt(samples)
    masked = jnp.where(dead_mask > 0, strain, jnp.zeros((), strain.dtype))
    lead = passed_along(masked[samples - HALF :], "win", 1)
    trail = passed_along(masked[:SPAN], "win", -1)
    rows = jnp.concatenate([lead, masked, trail], axis=0).astype(jnp.float32)
    sums = lax.reduce_window(
        jnp.abs(rows), jnp.zeros((), jnp.float32), lax.add, (2 * HALF + 1, 1), (1, 1), "VALID"
    )
    center = rows[HALF : rows.shape[0] - HALF]
    flat = (center / (sums / (2 * HALF + 1) + EPSILON)).astype(jnp.bfloat16)
    offset = lax.axis_index("src") * channels
    onehot = (src_index[:, None] - offset == jnp.arange(channels, dtype=jnp.int32)[None, :]).astype(
        jnp.bfloat16
    )
    selected = lax.dot_general(
        onehot, flat[:samples], (((1,), (1,)), ((), ())), preferred_element_type=jnp.float32
    )
    traces = lax.psum_scatter(
        selected.astype(jnp.bfloat16), "src", scatter_dimension=0, tiled=True
    )
    sources = traces.shape[0]
    tail = flat.shape[0] - samples
    shifted = [jnp.pad(traces, ((0, 0), (lag, tail - lag))) for lag in range(LAGS)]
    lagged = jnp.stack(shifted, axis=1).reshape(sources * LAGS, flat.shape[0])
    everywhere = lax.all_gather(flat, "src", axis=1, tiled=True)
    joined = jnp.dot(lagged, everywhere, preferred_element_type=jnp.float32) * scale
    return joined.reshape(1, sources, LAGS, channels * devices)


def lined(devices, channels):
    return devices == 8 and channels == sum(WIDTHS)


def shards(strain, dead_mask, src_index):
    if lined(lax.axis_size("src"), strain.shape[1]):
        return line_of_four(strain, dead_mask, src_index)
    return gathered(strain, dead_mask, src_index)


def solution(mesh):
    in_specs = (P("win", "src"), P("win", "src"), P())
    out_specs = P("win", "src", None, None)
    return jax.shard_map(shards, mesh=mesh, in_specs=in_specs, out_specs=out_specs, check_vma=False)
```

profile of v0, /device:TPU:8, one launch (start us, length us, event | category | flops | bytes accessed | tf_op | source)
XLA Modules:
  0.0 356.2 jit_solution(16554824681814149931)
XLA Ops:
  21.0 10.1 %collective-permute-done.2 = bf16[4,32,1536]{2,1,0:T(8,128)(2,1)} collective-permute-done((bf16[4,32,1536]{2,1,0:T(8,128)(2,1)}, bf16[4,32,1536]{2,1,0:T(8,128)(2,1)}, u32[]{:S(2)}, u32[]{:S(2)}) %collective-permute-start.2) | collective-permute-done | bytes 393248 | tf_op jit(solution)/shard_map/ppermute | solution.py:293
  38.3 5.7 %collective-permute-done.3 = bf16[32,1536]{1,0:T(8,128)(2,1)S(1)} collective-permute-done((bf16[32,1536]{1,0:T(8,128)(2,1)}, bf16[32,1536]{1,0:T(8,128)(2,1)S(1)}, u32[]{:S(2)}, u32[]{:S(2)}) %collective-permute-start.3) | collective-permute-done | bytes 98336 | tf_op jit(solution)/shard_map/ppermute | solution.py:293
  49.6 17.8 %collective-permute-done.6 = bf16[32,1536]{1,0:T(8,128)(2,1)S(1)} collective-permute-done((bf16[32,1536]{1,0:T(8,128)(2,1)S(1)}, bf16[32,1536]{1,0:T(8,128)(2,1)S(1)}, u32[]{:S(2)}, u32[]{:S(2)}) %collective-permute-start.6) | collective-permute-done | bytes 98336 | tf_op jit(solution)/shard_map/ppermute | solution.py:293
  67.4 3.5 collective-permute-start.23
  73.3 3.5 collective-permute-start.19
  78.1 3.4 correlate.13.refs_2_
  82.7 4.8 %correlate.14.refs_3_ = f32[1,32,32,10240]{3,2,1,0:T(8,128)} custom-call(s32[1]{0:T(128)} %bitcast.me_ref, bf16[1024,1664]{1,0:T(8,128)(2,1)S(1)} %hankel.2.refs_0_, bf16[1568,512]{1,0:T(8,128)(2,1)} %collective-permute-done.14.refs_1_, f32[1,32,32,10240]{3,2,1,0:T(8,128)} %correlate.13.refs_2_), custom_call_target="tpu_custom_call", output_to_operand_aliasing={{}: (3, {})} | custom-call | flops 1744830464 | bytes 3702784 | tf_op jit(solution)/shard_map/correlate/pallas_call | solution.py:240
  87.5 37.0 %collective-permute-done.16.refs_3_ = bf16[1568,256]{1,0:T(8,128)(2,1)S(1)} collective-permute-done((bf16[1568,256]{1,0:T(8,128)(2,1)}, bf16[1568,256]{1,0:T(8,128)(2,1)S(1)}, u32[]{:S(2)}, u32[]{:S(2)}) %collective-permute-start.16) | collective-permute-done | bytes 802848 | tf_op jit(solution)/shard_map/ppermute | solution.py:293
  125.8 5.7 %correlate.15 = (f32[1,32,32,10240]{3,2,1,0:T(8,128)}, bf16[32,32,512]{2,1,0:T(8,128)(2,1)S(1)}) custom-call(s32[1]{0:T(128)} %bitcast.me_ref, bf16[1024,1664]{1,0:T(8,128)(2,1)S(1)} %hankel.2.refs_0_, bf16[1024,1664]{1,0:T(8,128)(2,1)S(1)} %hankel.3.refs_1_, bf16[1568,512]{1,0:T(8,128)(2,1)S(1)} %normalize.4.refs_1_.refs_2_, ...), custom_call_target="tpu_custom_call", output_to_operand_aliasing={{0}: (4, {})} | custom-call | flops 3489660928 | bytes 3702784 | tf_op jit(solution)/shard_map/correlate/pallas_call | solution.py:240
  131.5 3.5 collective-permute-start.11
  136.6 3.5 correlate.16
  140.6 18.3 %collective-permute-done.19.refs_3_ = bf16[1568,512]{1,0:T(8,128)(2,1)S(1)} collective-permute-done((bf16[1568,512]{1,0:T(8,128)(2,1)S(1)}, bf16[1568,512]{1,0:T(8,128)(2,1)S(1)}, u32[]{:S(2)}, u32[]{:S(2)}) %collective-permute-start.19) | collective-permute-done | bytes 1605664 | tf_op jit(solution)/shard_map/ppermute | solution.py:293
  160.3 3.5 collective-permute-start.27
  163.8 5.7 %correlate.17 = (f32[1,32,32,10240]{3,2,1,0:T(8,128)}, bf16[32,32,512]{2,1,0:T(8,128)(2,1)S(1)}) custom-call(s32[1]{0:T(128)} %bitcast.me_ref, bf16[1024,1664]{1,0:T(8,128)(2,1)S(1)} %hankel.2.refs_0_, bf16[1024,1664]{1,0:T(8,128)(2,1)S(1)} %hankel.3.refs_1_, bf16[1568,512]{1,0:T(8,128)(2,1)S(1)} %collective-permute-done.10.refs_2_, ...), custom_call_target="tpu_custom_call", output_to_operand_aliasing={{0}: (4, {})} | custom-call | flops 3489660928 | bytes 3702784 | tf_op jit(solution)/shard_map/correlate/pallas_call | solution.py:240
  172.7 20.7 %collective-permute-done.11.refs_3_ = bf16[1568,512]{1,0:T(8,128)(2,1)} collective-permute-done((bf16[1568,512]{1,0:T(8,128)(2,1)S(1)}, bf16[1568,512]{1,0:T(8,128)(2,1)}, u32[]{:S(2)}, u32[]{:S(2)}) %collective-permute-start.11) | collective-permute-done | bytes 1605664 | tf_op jit(solution)/shard_map/ppermute | solution.py:293
  195.9 5.6 %correlate.18 = (f32[1,32,32,10240]{3,2,1,0:T(8,128)}, bf16[32,32,512]{2,1,0:T(8,128)(2,1)S(1)}) custom-call(s32[1]{0:T(128)} %bitcast.me_ref, bf16[1024,1664]{1,0:T(8,128)(2,1)S(1)} %hankel.2.refs_0_, bf16[1024,1664]{1,0:T(8,128)(2,1)S(1)} %hankel.3.refs_1_, bf16[1568,512]{1,0:T(8,128)(2,1)S(1)} %collective-permute-done.13.refs_2_, ...), custom_call_target="tpu_custom_call", output_to_operand_aliasing={{0}: (4, {})} | custom-call | flops 3489660928 | bytes 3702784 | tf_op jit(solution)/shard_map/correlate/pallas_call | solution.py:240
  203.1 4.7 %correlate.19 = (f32[1,32,32,10240]{3,2,1,0:T(8,128)}, bf16[32,32,256]{2,1,0:T(8,128)(2,1)S(1)}) custom-call(s32[1]{0:T(128)} %bitcast.me_ref, bf16[1024,1664]{1,0:T(8,128)(2,1)S(1)} %hankel.2.refs_0_, bf16[1024,1664]{1,0:T(8,128)(2,1)S(1)} %hankel.3.refs_1_, bf16[1568,256]{1,0:T(8,128)(2,1)} %collective-permute-done.7.refs_2_, ...), custom_call_target="tpu_custom_call", output_to_operand_aliasing={{0}: (4, {})} | custom-call | flops 1744830464 | bytes 1851392 | tf_op jit(solution)/shard_map/correlate/pallas_call | solution.py:240
  209.7 17.5 %collective-permute-done.27.refs_3_ = bf16[1568,512]{1,0:T(8,128)(2,1)} collective-permute-done((bf16[1568,512]{1,0:T(8,128)(2,1)S(1)}, bf16[1568,512]{1,0:T(8,128)(2,1)}, u32[]{:S(2)}, u32[]{:S(2)}) %collective-permute-start.27) | collective-permute-done | bytes 1605664 | tf_op jit(solution)/shard_map/ppermute | solution.py:293
  229.6 5.6 %correlate.20 = (f32[1,32,32,10240]{3,2,1,0:T(8,128)}, bf16[32,32,512]{2,1,0:T(8,128)(2,1)S(1)}) custom-call(s32[1]{0:T(128)} %bitcast.me_ref, bf16[1024,1664]{1,0:T(8,128)(2,1)S(1)} %hankel.2.refs_0_, bf16[1024,1664]{1,0:T(8,128)(2,1)S(1)} %hankel.3.refs_1_, bf16[1568,512]{1,0:T(8,128)(2,1)S(1)} %collective-permute-done.24.refs_2_, ...), custom_call_target="tpu_custom_call", output_to_operand_aliasing={{0}: (5, {})} | custom-call | flops 3489660928 | bytes 3702784 | tf_op jit(solution)/shard_map/correlate/pallas_call | solution.py:240
  237.6 3.5 collective-permute-start.8
  242.7 5.6 %correlate.21 = (f32[1,32,32,10240]{3,2,1,0:T(8,128)}, bf16[32,32,512]{2,1,0:T(8,128)(2,1)S(1)}) custom-call(s32[1]{0:T(128)} %bitcast.me_ref, bf16[1024,1664]{1,0:T(8,128)(2,1)S(1)} %hankel.2.refs_0_, bf16[1024,1664]{1,0:T(8,128)(2,1)S(1)} %hankel.3.refs_1_, bf16[1568,512]{1,0:T(8,128)(2,1)S(1)} %collective-permute-done.20.refs_2_, ...), custom_call_target="tpu_custom_call", output_to_operand_aliasing={{0}: (5, {})} | custom-call | flops 3489660928 | bytes 3702784 | tf_op jit(solution)/shard_map/correlate/pallas_call | solution.py:240
  251.0 3.5 correlate.22
  255.5 9.1 %collective-permute-done.12.refs_2_ = bf16[1568,512]{1,0:T(8,128)(2,1)} collective-permute-done((bf16[1568,512]{1,0:T(8,128)(2,1)}, bf16[1568,512]{1,0:T(8,128)(2,1)}, u32[]{:S(2)}, u32[]{:S(2)}) %collective-permute-start.12) | collective-permute-done | bytes 1605664 | tf_op jit(solution)/shard_map/ppermute | solution.py:293
  266.1 7.6 %correlate.23 = (f32[1,32,32,10240]{3,2,1,0:T(8,128)}, bf16[32,32,512]{2,1,0:T(8,128)(2,1)S(1)}) custom-call(s32[1]{0:T(128)} %bitcast.me_ref, bf16[1024,1664]{1,0:T(8,128)(2,1)S(1)} %hankel.2.refs_0_, bf16[1024,1664]{1,0:T(8,128)(2,1)S(1)} %hankel.3.refs_1_, bf16[1568,512]{1,0:T(8,128)(2,1)} %collective-permute-done.12.refs_2_, ...), custom_call_target="tpu_custom_call", output_to_operand_aliasing={{0}: (5, {})} | custom-call | flops 3489660928 | bytes 3702784 | tf_op jit(solution)/shard_map/correlate/pallas_call | solution.py:240
  274.2 4.4 %collective-permute-start.9 = (bf16[1568,256]{1,0:T(8,128)(2,1)S(1)}, bf16[1568,256]{1,0:T(8,128)(2,1)S(1)}, u32[]{:S(2)}, u32[]{:S(2)}) collective-permute-start(bf16[1568,256]{1,0:T(8,128)(2,1)S(1)} %collective-permute-done.8.refs_3_), channel_id=1, source_target_pairs={{2,0},{3,1},{4,6},{5,7},{10,8},{11,9},{12,14},{13,15},{18,16},{19,... | collective-permute-start | bytes 2408456 | tf_op jit(solution)/shard_map/ppermute | solution.py:293
  280.0 9.7 %collective-permute-done.30.got_ref = bf16[32,32,512]{2,1,0:T(8,128)(2,1)S(1)} collective-permute-done((bf16[32,32,512]{2,1,0:T(8,128)(2,1)S(1)}, bf16[32,32,512]{2,1,0:T(8,128)(2,1)S(1)}, u32[]{:S(2)}, u32[]{:S(2)}) %collective-permute-start.30) | collective-permute-done | bytes 1048608 | tf_op jit(solution)/shard_map/ppermute | solution.py:293
  291.1 9.8 %collective-permute-done.29.got_ref = bf16[32,32,256]{2,1,0:T(8,128)(2,1)S(1)} collective-permute-done((bf16[32,32,256]{2,1,0:T(8,128)(2,1)S(1)}, bf16[32,32,256]{2,1,0:T(8,128)(2,1)S(1)}, u32[]{:S(2)}, u32[]{:S(2)}) %collective-permute-start.29) | collective-permute-done | bytes 524320 | tf_op jit(solution)/shard_map/ppermute | solution.py:293
  301.9 7.6 %correlate.24 = (f32[1,32,32,10240]{3,2,1,0:T(8,128)}, bf16[32,32,512]{2,1,0:T(8,128)(2,1)S(1)}) custom-call(s32[1]{0:T(128)} %bitcast.me_ref, bf16[1024,1664]{1,0:T(8,128)(2,1)S(1)} %hankel.2.refs_0_, bf16[1024,1664]{1,0:T(8,128)(2,1)S(1)} %hankel.3.refs_1_, bf16[1568,512]{1,0:T(8,128)(2,1)} %collective-permute-done.28.refs_2_, ...), custom_call_target="tpu_custom_call", output_to_operand_aliasing={{0}: (5, {})} | custom-call | flops 3489660928 | bytes 3702784 | tf_op jit(solution)/shard_map/correlate/pallas_call | solution.py:240
  311.0 12.4 %collective-permute-done.26.got_ref = bf16[32,32,512]{2,1,0:T(8,128)(2,1)S(1)} collective-permute-done((bf16[32,32,512]{2,1,0:T(8,128)(2,1)S(1)}, bf16[32,32,512]{2,1,0:T(8,128)(2,1)S(1)}, u32[]{:S(2)}, u32[]{:S(2)}) %collective-permute-start.26) | collective-permute-done | bytes 1048608 | tf_op jit(solution)/shard_map/ppermute | solution.py:293
  324.8 3.5 correlate.25
  329.8 16.0 %collective-permute-done.33.got_ref = bf16[32,32,512]{2,1,0:T(8,128)(2,1)S(1)} collective-permute-done((bf16[32,32,512]{2,1,0:T(8,128)(2,1)S(1)}, bf16[32,32,512]{2,1,0:T(8,128)(2,1)S(1)}, u32[]{:S(2)}, u32[]{:S(2)}) %collective-permute-start.33) | collective-permute-done | bytes 1048608 | tf_op jit(solution)/shard_map/ppermute | solution.py:293
  347.2 8.0 %collective-permute-done.32.got_ref = bf16[32,32,256]{2,1,0:T(8,128)(2,1)S(1)} collective-permute-done((bf16[32,32,256]{2,1,0:T(8,128)(2,1)S(1)}, bf16[32,32,256]{2,1,0:T(8,128)(2,1)S(1)}, u32[]{:S(2)}, u32[]{:S(2)}) %collective-permute-start.32) | collective-permute-done | bytes 524320 | tf_op jit(solution)/shard_map/ppermute | solution.py:293
  (101 shorter events, 75.2 us)
Async XLA Ops:
  18.9 12.2 %collective-permute-start.2 = (bf16[4,32,1536]{2,1,0:T(8,128)(2,1)}, bf16[4,32,1536]{2,1,0:T(8,128)(2,1)}, u32[]{:S(2)}, u32[]{:S(2)}) collective-permute-start(bf16[4,32,1536]{2,1,0:T(8,128)(2,1)} %dynamic-slice_bitcast_fusion), channel_id=1, source_target_pairs={{0,1},{1,0},{2,3},{3,2},{4,5},{5,4},{6,7},{7,6},{8,9},{9,8},{10,11... | collective-permute-start | bytes 1179656 | tf_op jit(solution)/shard_map/ppermute | solution.py:293
  20.4 52.9 %collective-permute-start.14 = (bf16[1568,512]{1,0:T(8,128)(2,1)S(1)}, bf16[1568,512]{1,0:T(8,128)(2,1)}, u32[]{:S(2)}, u32[]{:S(2)}) collective-permute-start(bf16[1568,512]{1,0:T(8,128)(2,1)S(1)} %normalize.3.refs_0_.refs_1_), channel_id=1, source_target_pairs={{0,1},{1,0},{2,3},{3,2},{4,5},{5,4},{6,7},{7,6},{8,9},{9,8},{10,11... | collective-permute-start | bytes 4816904 | tf_op jit(solution)/shard_map/ppermute | solution.py:293
  20.9 50.0 %collective-permute-start.7 = (bf16[1568,256]{1,0:T(8,128)(2,1)}, bf16[1568,256]{1,0:T(8,128)(2,1)}, u32[]{:S(2)}, u32[]{:S(2)}) collective-permute-start(bf16[1568,256]{1,0:T(8,128)(2,1)} %copy-done.1), channel_id=1, source_target_pairs={{0,2},{1,3},{2,0},{3,1},{4,6},{5,7},{6,4},{7,5},{8,10},{9,11},{10,... | collective-permute-start | bytes 2408456 | tf_op jit(solution)/shard_map/ppermute | solution.py:293
  33.7 10.3 %collective-permute-start.3 = (bf16[32,1536]{1,0:T(8,128)(2,1)}, bf16[32,1536]{1,0:T(8,128)(2,1)S(1)}, u32[]{:S(2)}, u32[]{:S(2)}) collective-permute-start(bf16[32,1536]{1,0:T(8,128)(2,1)} %get-tuple-element.49), channel_id=1, source_target_pairs={{0,2},{1,3},{2,4},{3,5},{4,6},{5,7},{6,0},{7,1},{8,10},{9,11},{10,... | collective-permute-start | bytes 294920 | tf_op jit(solution)/shard_map/ppermute | solution.py:293
  35.2 11.9 %collective-permute-start.4 = (bf16[32,1536]{1,0:T(8,128)(2,1)}, bf16[32,1536]{1,0:T(8,128)(2,1)S(1)}, u32[]{:S(2)}, u32[]{:S(2)}) collective-permute-start(bf16[32,1536]{1,0:T(8,128)(2,1)} %get-tuple-element.51), channel_id=1, source_target_pairs={{0,4},{1,5},{2,6},{3,7},{4,0},{5,1},{6,2},{7,3},{8,12},{9,13},{10,... | collective-permute-start | bytes 294920 | tf_op jit(solution)/shard_map/ppermute | solution.py:293
  36.2 10.9 %collective-permute-start.5 = (bf16[32,1536]{1,0:T(8,128)(2,1)}, bf16[32,1536]{1,0:T(8,128)(2,1)S(1)}, u32[]{:S(2)}, u32[]{:S(2)}) collective-permute-start(bf16[32,1536]{1,0:T(8,128)(2,1)} %get-tuple-element.50), channel_id=1, source_target_pairs={{0,6},{1,7},{2,0},{3,1},{4,2},{5,3},{6,4},{7,5},{8,14},{9,15},{10,... | collective-permute-start | bytes 294920 | tf_op jit(solution)/shard_map/ppermute | solution.py:293
  44.0 87.5 %collective-permute-start.10 = (bf16[1568,512]{1,0:T(8,128)(2,1)S(1)}, bf16[1568,512]{1,0:T(8,128)(2,1)S(1)}, u32[]{:S(2)}, u32[]{:S(2)}) collective-permute-start(bf16[1568,512]{1,0:T(8,128)(2,1)S(1)} %normalize.3.refs_0_.refs_1_), channel_id=1, source_target_pairs={{0,2},{1,3},{2,0},{3,1},{4,6},{5,7},{6,4},{7,5},{8,10},{9,11},{10,... | collective-permute-start | bytes 4816904 | tf_op jit(solution)/shard_map/ppermute | solution.py:293
  47.1 87.9 %collective-permute-start.13 = (bf16[1568,512]{1,0:T(8,128)(2,1)S(1)}, bf16[1568,512]{1,0:T(8,128)(2,1)S(1)}, u32[]{:S(2)}, u32[]{:S(2)}) collective-permute-start(bf16[1568,512]{1,0:T(8,128)(2,1)S(1)} %normalize.4.refs_1_.refs_2_), channel_id=1, source_target_pairs={{0,2},{1,3},{2,0},{3,1},{4,6},{5,7},{6,4},{7,5},{8,10},{9,11},{10,... | collective-permute-start | bytes 4816904 | tf_op jit(solution)/shard_map/ppermute | solution.py:293
  48.0 19.4 %collective-permute-start.6 = (bf16[32,1536]{1,0:T(8,128)(2,1)S(1)}, bf16[32,1536]{1,0:T(8,128)(2,1)S(1)}, u32[]{:S(2)}, u32[]{:S(2)}) collective-permute-start(bf16[32,1536]{1,0:T(8,128)(2,1)S(1)} %fusion.1), channel_id=1, source_target_pairs={{0,1},{1,0},{2,3},{3,2},{4,5},{5,4},{6,7},{7,6},{8,9},{9,8},{10,11... | collective-permute-start | bytes 294920 | tf_op jit(solution)/shard_map/ppermute | solution.py:293
  67.4 72.7 %collective-permute-start.23 = (bf16[1568,512]{1,0:T(8,128)(2,1)S(1)}, bf16[1568,512]{1,0:T(8,128)(2,1)S(1)}, u32[]{:S(2)}, u32[]{:S(2)}) collective-permute-start(bf16[1568,512]{1,0:T(8,128)(2,1)S(1)} %normalize.3.refs_0_.refs_1_), channel_id=1, source_target_pairs={{2,4},{3,5},{4,2},{5,3},{10,12},{11,13},{12,10},{13,11},{18,20},{1... | collective-permute-start | bytes 4816904 | tf_op jit(solution)/shard_map/ppermute | solution.py:293
  70.9 53.6 %collective-permute-start.16 = (bf16[1568,256]{1,0:T(8,128)(2,1)}, bf16[1568,256]{1,0:T(8,128)(2,1)S(1)}, u32[]{:S(2)}, u32[]{:S(2)}) collective-permute-start(bf16[1568,256]{1,0:T(8,128)(2,1)} %copy-done.1), channel_id=1, source_target_pairs={{2,4},{3,5},{4,2},{5,3},{10,12},{11,13},{12,10},{13,11},{18,20},{1... | collective-permute-start | bytes 2408456 | tf_op jit(solution)/shard_map/ppermute | solution.py:293
  73.3 85.6 %collective-permute-start.19 = (bf16[1568,512]{1,0:T(8,128)(2,1)S(1)}, bf16[1568,512]{1,0:T(8,128)(2,1)S(1)}, u32[]{:S(2)}, u32[]{:S(2)}) collective-permute-start(bf16[1568,512]{1,0:T(8,128)(2,1)S(1)} %normalize.4.refs_1_.refs_2_), channel_id=1, source_target_pairs={{2,4},{3,5},{4,2},{5,3},{10,12},{11,13},{12,10},{13,11},{18,20},{1... | collective-permute-start | bytes 4816904 | tf_op jit(solution)/shard_map/ppermute | solution.py:293
  124.5 35.8 %collective-permute-start.17 = (bf16[1568,256]{1,0:T(8,128)(2,1)S(1)}, bf16[1568,256]{1,0:T(8,128)(2,1)S(1)}, u32[]{:S(2)}, u32[]{:S(2)}) collective-permute-start(bf16[1568,256]{1,0:T(8,128)(2,1)S(1)} %collective-permute-done.16.refs_3_), channel_id=1, source_target_pairs={{2,0},{3,1},{4,6},{5,7},{10,8},{11,9},{12,14},{13,15},{18,16},{19,... | collective-permute-start | bytes 2408456 | tf_op jit(solution)/shard_map/ppermute | solution.py:293
  131.5 61.9 %collective-permute-start.11 = (bf16[1568,512]{1,0:T(8,128)(2,1)S(1)}, bf16[1568,512]{1,0:T(8,128)(2,1)}, u32[]{:S(2)}, u32[]{:S(2)}) collective-permute-start(bf16[1568,512]{1,0:T(8,128)(2,1)S(1)} %collective-permute-done.10.refs_2_), channel_id=1, source_target_pairs={{2,4},{3,5},{4,2},{5,3},{10,12},{11,13},{12,10},{13,11},{18,20},{1... | collective-permute-start | bytes 4816904 | tf_op jit(solution)/shard_map/ppermute | solution.py:293
  135.0 36.3 %collective-permute-start.25 = (bf16[32,32,512]{2,1,0:T(8,128)(2,1)S(1)}, bf16[32,32,512]{2,1,0:T(8,128)(2,1)S(1)}, u32[]{:S(2)}, u32[]{:S(2)}) collective-permute-start(bf16[32,32,512]{2,1,0:T(8,128)(2,1)S(1)} %get-tuple-element.35), channel_id=1, source_target_pairs={{0,1},{1,0},{2,3},{3,2},{4,5},{5,4},{6,7},{7,6},{8,9},{9,8},{10,11... | collective-permute-start | bytes 3145736 | tf_op jit(solution)/shard_map/ppermute | solution.py:293
  140.1 29.6 %collective-permute-start.22 = (bf16[32,32,256]{2,1,0:T(8,128)(2,1)S(1)}, bf16[32,32,256]{2,1,0:T(8,128)(2,1)S(1)}, u32[]{:S(2)}, u32[]{:S(2)}) collective-permute-start(bf16[32,32,256]{2,1,0:T(8,128)(2,1)S(1)} %get-tuple-element.34), channel_id=1, source_target_pairs={{0,1},{1,0},{2,3},{3,2},{4,5},{5,4},{6,7},{7,6},{8,9},{9,8},{10,11... | collective-permute-start | bytes 1572872 | tf_op jit(solution)/shard_map/ppermute | solution.py:293
  158.9 48.8 %collective-permute-start.24 = (bf16[1568,512]{1,0:T(8,128)(2,1)S(1)}, bf16[1568,512]{1,0:T(8,128)(2,1)S(1)}, u32[]{:S(2)}, u32[]{:S(2)}) collective-permute-start(bf16[1568,512]{1,0:T(8,128)(2,1)S(1)} %collective-permute-done.23.refs_3_), channel_id=1, source_target_pairs={{2,0},{3,1},{4,6},{5,7},{10,8},{11,9},{12,14},{13,15},{18,16},{19,... | collective-permute-start | bytes 4816904 | tf_op jit(solution)/shard_map/ppermute | solution.py:293
  160.3 66.8 %collective-permute-start.27 = (bf16[1568,512]{1,0:T(8,128)(2,1)S(1)}, bf16[1568,512]{1,0:T(8,128)(2,1)}, u32[]{:S(2)}, u32[]{:S(2)}) collective-permute-start(bf16[1568,512]{1,0:T(8,128)(2,1)S(1)} %collective-permute-done.13.refs_2_), channel_id=1, source_target_pairs={{2,4},{3,5},{4,2},{5,3},{10,12},{11,13},{12,10},{13,11},{18,20},{1... | collective-permute-start | bytes 4816904 | tf_op jit(solution)/shard_map/ppermute | solution.py:293
  169.8 31.8 %collective-permute-start.21 = (bf16[32,32,512]{2,1,0:T(8,128)(2,1)S(1)}, bf16[32,32,512]{2,1,0:T(8,128)(2,1)S(1)}, u32[]{:S(2)}, u32[]{:S(2)}) collective-permute-start(bf16[32,32,512]{2,1,0:T(8,128)(2,1)S(1)} %get-tuple-element.33), channel_id=1, source_target_pairs={{0,1},{1,0},{2,3},{3,2},{4,5},{5,4},{6,7},{7,6},{8,9},{9,8},{10,11... | collective-permute-start | bytes 3145736 | tf_op jit(solution)/shard_map/ppermute | solution.py:293
  171.3 69.8 %collective-permute-start.20 = (bf16[1568,512]{1,0:T(8,128)(2,1)S(1)}, bf16[1568,512]{1,0:T(8,128)(2,1)S(1)}, u32[]{:S(2)}, u32[]{:S(2)}) collective-permute-start(bf16[1568,512]{1,0:T(8,128)(2,1)S(1)} %collective-permute-done.19.refs_3_), channel_id=1, source_target_pairs={{2,0},{3,1},{4,6},{5,7},{10,8},{11,9},{12,14},{13,15},{18,16},{19,... | collective-permute-start | bytes 4816904 | tf_op jit(solution)/shard_map/ppermute | solution.py:293
  193.4 71.2 %collective-permute-start.12 = (bf16[1568,512]{1,0:T(8,128)(2,1)}, bf16[1568,512]{1,0:T(8,128)(2,1)}, u32[]{:S(2)}, u32[]{:S(2)}) collective-permute-start(bf16[1568,512]{1,0:T(8,128)(2,1)} %collective-permute-done.11.refs_3_), channel_id=1, source_target_pairs={{2,0},{3,1},{4,6},{5,7},{10,8},{11,9},{12,14},{13,15},{18,16},{19,... | collective-permute-start | bytes 4816904 | tf_op jit(solution)/shard_map/ppermute | solution.py:293
  201.6 46.8 %collective-permute-start.18 = (bf16[32,32,512]{2,1,0:T(8,128)(2,1)S(1)}, bf16[32,32,512]{2,1,0:T(8,128)(2,1)S(1)}, u32[]{:S(2)}, u32[]{:S(2)}) collective-permute-start(bf16[32,32,512]{2,1,0:T(8,128)(2,1)S(1)} %get-tuple-element.32), channel_id=1, source_target_pairs={{0,1},{1,0},{2,3},{3,2},{4,5},{5,4},{6,7},{7,6},{8,9},{9,8},{10,11... | collective-permute-start | bytes 3145736 | tf_op jit(solution)/shard_map/ppermute | solution.py:293
  207.8 29.9 %collective-permute-start.15 = (bf16[32,32,256]{2,1,0:T(8,128)(2,1)S(1)}, bf16[32,32,256]{2,1,0:T(8,128)(2,1)S(1)}, u32[]{:S(2)}, u32[]{:S(2)}) collective-permute-start(bf16[32,32,256]{2,1,0:T(8,128)(2,1)S(1)} %get-tuple-element.31), channel_id=1, source_target_pairs={{0,1},{1,0},{2,3},{3,2},{4,5},{5,4},{6,7},{7,6},{8,9},{9,8},{10,11... | collective-permute-start | bytes 1572872 | tf_op jit(solution)/shard_map/ppermute | solution.py:293
  227.1 74.8 %collective-permute-start.28 = (bf16[1568,512]{1,0:T(8,128)(2,1)}, bf16[1568,512]{1,0:T(8,128)(2,1)}, u32[]{:S(2)}, u32[]{:S(2)}) collective-permute-start(bf16[1568,512]{1,0:T(8,128)(2,1)} %collective-permute-done.27.refs_3_), channel_id=1, source_target_pairs={{2,0},{3,1},{4,6},{5,7},{10,8},{11,9},{12,14},{13,15},{18,16},{19,... | collective-permute-start | bytes 4816904 | tf_op jit(solution)/shard_map/ppermute | solution.py:293
  237.6 36.0 %collective-permute-start.8 = (bf16[1568,256]{1,0:T(8,128)(2,1)}, bf16[1568,256]{1,0:T(8,128)(2,1)S(1)}, u32[]{:S(2)}, u32[]{:S(2)}) collective-permute-start(bf16[1568,256]{1,0:T(8,128)(2,1)} %collective-permute-done.7.refs_2_), channel_id=1, source_target_pairs={{2,4},{3,5},{4,2},{5,3},{10,12},{11,13},{12,10},{13,11},{18,20},{1... | collective-permute-start | bytes 2408456 | tf_op jit(solution)/shard_map/ppermute | solution.py:293
  241.1 33.1 %collective-permute-start.31 = (bf16[32,32,512]{2,1,0:T(8,128)(2,1)S(1)}, bf16[32,32,512]{2,1,0:T(8,128)(2,1)S(1)}, u32[]{:S(2)}, u32[]{:S(2)}) collective-permute-start(bf16[32,32,512]{2,1,0:T(8,128)(2,1)S(1)} %get-tuple-element.43), channel_id=1, source_target_pairs={{0,1},{1,0},{2,3},{3,2},{4,5},{5,4},{6,7},{7,6},{8,9},{9,8},{10,11... | collective-permute-start | bytes 3145736 | tf_op jit(solution)/shard_map/ppermute | solution.py:293
  248.3 41.3 %collective-permute-start.30 = (bf16[32,32,512]{2,1,0:T(8,128)(2,1)S(1)}, bf16[32,32,512]{2,1,0:T(8,128)(2,1)S(1)}, u32[]{:S(2)}, u32[]{:S(2)}) collective-permute-start(bf16[32,32,512]{2,1,0:T(8,128)(2,1)S(1)} %get-tuple-element.42), channel_id=1, source_target_pairs={{0,1},{1,0},{2,3},{3,2},{4,5},{5,4},{6,7},{7,6},{8,9},{9,8},{10,11... | collective-permute-start | bytes 3145736 | tf_op jit(solution)/shard_map/ppermute | solution.py:293
  264.6 36.3 %collective-permute-start.29 = (bf16[32,32,256]{2,1,0:T(8,128)(2,1)S(1)}, bf16[32,32,256]{2,1,0:T(8,128)(2,1)S(1)}, u32[]{:S(2)}, u32[]{:S(2)}) collective-permute-start(bf16[32,32,256]{2,1,0:T(8,128)(2,1)S(1)} %get-tuple-element.41), channel_id=1, source_target_pairs={{0,1},{1,0},{2,3},{3,2},{4,5},{5,4},{6,7},{7,6},{8,9},{9,8},{10,11... | collective-permute-start | bytes 1572872 | tf_op jit(solution)/shard_map/ppermute | solution.py:293
  273.7 49.7 %collective-permute-start.26 = (bf16[32,32,512]{2,1,0:T(8,128)(2,1)S(1)}, bf16[32,32,512]{2,1,0:T(8,128)(2,1)S(1)}, u32[]{:S(2)}, u32[]{:S(2)}) collective-permute-start(bf16[32,32,512]{2,1,0:T(8,128)(2,1)S(1)} %get-tuple-element.40), channel_id=1, source_target_pairs={{0,1},{1,0},{2,3},{3,2},{4,5},{5,4},{6,7},{7,6},{8,9},{9,8},{10,11... | collective-permute-start | bytes 3145736 | tf_op jit(solution)/shard_map/ppermute | solution.py:293
  274.2 50.6 %collective-permute-start.9 = (bf16[1568,256]{1,0:T(8,128)(2,1)S(1)}, bf16[1568,256]{1,0:T(8,128)(2,1)S(1)}, u32[]{:S(2)}, u32[]{:S(2)}) collective-permute-start(bf16[1568,256]{1,0:T(8,128)(2,1)S(1)} %collective-permute-done.8.refs_3_), channel_id=1, source_target_pairs={{2,0},{3,1},{4,6},{5,7},{10,8},{11,9},{12,14},{13,15},{18,16},{19,... | collective-permute-start | bytes 2408456 | tf_op jit(solution)/shard_map/ppermute | solution.py:293
  309.5 36.4 %collective-permute-start.33 = (bf16[32,32,512]{2,1,0:T(8,128)(2,1)S(1)}, bf16[32,32,512]{2,1,0:T(8,128)(2,1)S(1)}, u32[]{:S(2)}, u32[]{:S(2)}) collective-permute-start(bf16[32,32,512]{2,1,0:T(8,128)(2,1)S(1)} %get-tuple-element.47), channel_id=1, source_target_pairs={{0,1},{1,0},{2,3},{3,2},{4,5},{5,4},{6,7},{7,6},{8,9},{9,8},{10,11... | collective-permute-start | bytes 3145736 | tf_op jit(solution)/shard_map/ppermute | solution.py:293
  328.3 26.9 %collective-permute-start.32 = (bf16[32,32,256]{2,1,0:T(8,128)(2,1)S(1)}, bf16[32,32,256]{2,1,0:T(8,128)(2,1)S(1)}, u32[]{:S(2)}, u32[]{:S(2)}) collective-permute-start(bf16[32,32,256]{2,1,0:T(8,128)(2,1)S(1)} %get-tuple-element.46), channel_id=1, source_target_pairs={{0,1},{1,0},{2,3},{3,2},{4,5},{5,4},{6,7},{7,6},{8,9},{9,8},{10,11... | collective-permute-start | bytes 1572872 | tf_op jit(solution)/shard_map/ppermute | solution.py:293
  (14 other events, 101.7 us)
where the time goes:
time: 357 us; the launch traced here: 356 us
  waiting for transfers between devices  193 us (54%)
  Pallas kernels  88.1 us (25%)
  starting transfers between devices  61.2 us (17%)
  local copies, waits for them, and re-layouts  8.28 us (2%)
  other arithmetic  5.34 us (1%)
    ppermute x32, waiting for transfers between devices, hop(): return lax.ppermute(array, 'src', pairs)  193 us
    pallas_call x13, Pallas kernels, correlate(): pl.pallas_call(functools.partial(correlate_kernel, rows, len(operands) ==...  66.8 us
    ppermute x32, starting transfers between devices, hop(): return lax.ppermute(array, 'src', pairs)  56.8 us
    pallas_call x11, Pallas kernels, store(): pl.pallas_call(store_kernel, out_shape=jax.ShapeDtypeStruct(out.shape, ou...  13.7 us
  transfers between devices with their start and end apart: 34, of which 15 were waited for; matrix products, arithmetic and copies ran while one was open for 1% of the time, Pallas kernels for 23%

commit v1 on v0

--- a/solution.py
+++ b/solution.py
@@ -15,10 +15,18 @@
 TILE = 192
 SPAN = 2 * HALF
 ROWS = 512
-WIDTHS = (512, 512, 256)
-FLAT_SENT = 1
 VMEM_BYTES = 24 << 20
-LAG = (4, 4, 3, 1)
+
+WIDTHS = (384, 512, 256, 128)
+EARLY = (0, 1, 2, 3)
+LATE = (1, 0, 2, 3)
+STEPS = (
+    [(0, c) for c in EARLY[1:]]
+    + [(1, c) for c in EARLY]
+    + [(2, c) for c in LATE]
+    + [(3, c) for c in LATE]
+)
+STORED = {(1, 3): 4, (2, 1): 3, (2, 2): 1, (2, 3): 3, (3, 0): 1}
 
 
 def passed_along(array, axis, by):
@@ -27,14 +35,11 @@
     return lax.ppermute(array, axis, pairs)
 
 
-def normalize_kernel(strain_ref, mask_ref, lead_ref, trail_ref, flat_ref, rows):
-    samples = strain_ref.shape[0]
-    width = strain_ref.shape[1]
-    alive = jnp.broadcast_to(mask_ref[...] > 0, (samples, width))
+def normalize_kernel(offset, masked_ref, lead_ref, trail_ref, flat_ref, rows):
+    samples = masked_ref.shape[0]
+    columns = pl.ds(offset, flat_ref.shape[1])
+    pltpu.sync_copy(masked_ref.at[:, columns], rows.at[pl.ds(HALF, samples)])
     rows[:HALF] = lead_ref[...]
-    rows[HALF : HALF + samples] = jnp.where(
-        alive, strain_ref[...].astype(jnp.float32), 0.0
-    ).astype(jnp.bfloat16)
     rows[HALF + samples :] = trail_ref[...]
     out_rows = flat_ref.shape[0]
     row = lax.broadcasted_iota(jnp.int32, (TILE, TILE + SPAN), 0)
@@ -56,17 +61,17 @@
     return pltpu.CompilerParams(vmem_limit_bytes=VMEM_BYTES)
 
 
-def normalize_chunk(strain, mask, lead, trail, offset, width):
-    samples = strain.shape[0]
+def normalize_chunk(masked, lead, trail, offset, width):
+    samples = masked.shape[0]
 
     def block(rows):
         return pl.BlockSpec((pl.Element(rows), pl.Element(width)), lambda i: (0, offset))
 
     return pl.pallas_call(
-        normalize_kernel,
+        functools.partial(normalize_kernel, offset),
         out_shape=jax.ShapeDtypeStruct((samples + HALF, width), jnp.bfloat16),
         grid=(1,),
-        in_specs=[block(samples), block(1), block(HALF), block(SPAN)],
+        in_specs=[pl.BlockSpec(memory_space=pltpu.HBM), block(HALF), block(SPAN)],
         out_specs=pl.BlockSpec((samples + HALF, width), lambda i: (0, 0)),
         scratch_shapes=[pltpu.VMEM((samples + HALF + SPAN, width), jnp.bfloat16)],
         compiler_params=params(),
@@ -76,7 +81,7 @@
             transcendentals=0,
         ),
         name="normalize",
-    )(strain, mask, lead, trail)
+    )(masked, lead, trail)
 
 
 def select_kernel(index_ref, *refs):
@@ -318,10 +323,11 @@
 
     lead = passed_along(masked(strain[samples - HALF :]), "win", 1)
     trail = passed_along(masked(strain[:SPAN]), "win", -1)
+    alive = masked(strain)
     flats = []
     for c in range(count):
         flats.append(
-            normalize_chunk(strain, dead_mask, lead, trail, offsets[c], WIDTHS[c])
+            normalize_chunk(alive, lead, trail, offsets[c], WIDTHS[c])
         )
 
     selected = select_sources(flats, src_index - me * channels, samples)
@@ -342,7 +348,7 @@
 
     first_out = hops(flats, outer)
     first_in = hops(flats, inner)
-    swapped = hops(flats[:FLAT_SENT], across)
+    swapped = hop(flats[0], across)
     second_out = hops(first_in, outward)
     second_in = hops(first_out, inner)
     third_out = hops(second_in, outward)
@@ -360,28 +366,27 @@
     def place(slot, c, partner):
         return lambda me: (origin(slot, me) ^ partner) * channels + offsets[c]
 
-    for slot in range(line):
-        for c in range(count):
-            if slot == 0 and c < FLAT_SENT:
-                for partner, chunk in ((0, flats[c]), (1, swapped[c])):
-                    (out,) = correlate(
-                        [own_rows], [chunk], here, place(slot, c, partner), scale, out, total
-                    )
-                continue
-            out, made = correlate(
-                [own_rows, partner_rows],
-                arrivals[slot][c],
-                here,
-                place(slot, c, 0),
-                scale,
-                out,
-                total,
-            )
-            waiting.append((hop(made, across), here, place(slot, c, 1)))
-            while len(waiting) > LAG[slot]:
-                out = store(*waiting.pop(0), out)
+    def add(slot, c, partner, chunk, hankels):
+        nonlocal out
+        out, *sent = correlate(
+            hankels, chunk, here, place(slot, c, partner), scale, out, total
+        )
+        return sent
+
+    def keep():
+        nonlocal out
+        out = store(*waiting.pop(0), out)
+
+    add(0, 0, 0, [flats[0]], [own_rows])
+    for slot, c in STEPS:
+        (made,) = add(slot, c, 0, arrivals[slot][c], [own_rows, partner_rows])
+        waiting.append((hop(made, across), here, place(slot, c, 1)))
+        if (slot, c) == (0, count - 1):
+            add(0, 0, 1, [swapped], [own_rows])
+        for _ in range(STORED.get((slot, c), 0)):
+            keep()
     while waiting:
-        out = store(*waiting.pop(0), out)
+        keep()
     return out
 
 

time: 357 us -> 374 us (1.048)
  the two profiles are of different devices: /device:TPU:8 before, /device:TPU:16 now
where the time goes in v1:
time: 374 us; the launch traced here: 373 us
  waiting for transfers between devices  181 us (48%)
  Pallas kernels  105 us (28%)
  starting transfers between devices  68.4 us (18%)
  other arithmetic  10.4 us (3%)
  local copies, waits for them, and re-layouts  7.72 us (2%)
    ppermute x41, waiting for transfers between devices, hop(): return lax.ppermute(array, 'src', pairs)  181 us
    pallas_call x17, Pallas kernels, correlate(): pl.pallas_call(functools.partial(correlate_kernel, rows, len(operands) ==...  79.8 us
    ppermute x41, starting transfers between devices, hop(): return lax.ppermute(array, 'src', pairs)  64.1 us
    pallas_call x15, Pallas kernels, store(): pl.pallas_call(store_kernel, out_shape=jax.ShapeDtypeStruct(out.shape, ou...  16.4 us
  transfers between devices with their start and end apart: 43, of which 16 were waited for; matrix products, arithmetic and copies ran while one was open for 2% of the time, Pallas kernels for 26%

profile of v1, /device:TPU:16, one launch (start us, length us, event | category | flops | bytes accessed | tf_op | source)
XLA Modules:
  0.0 372.7 jit_solution(8370895418377115699)
XLA Ops:
  6.9 4.3 %broadcast_select_fusion.masked_ref = bf16[1536,1280]{1,0:T(8,128)(2,1)} fusion(bf16[1536,1280]{1,0:T(8,128)(2,1)} %param.3, pred[1280]{0:T(1024)(128)(4,1)S(1)} %compare_reduce_fusion), kind=kLoop, calls=%fused_computation | loop fusion | flops 1966080 | bytes 7865600 | tf_op jit(solution)/shard_map/jit(_where)/select_n | solution.py:322
  19.1 3.8 %select.3 = bf16[256,1536]{1,0:T(8,128)(2,1)} custom-call(s32[256,1]{1,0:T(8,128)S(1)} %copy-done.7, bf16[1568,384]{1,0:T(8,128)(2,1)S(1)} %normalize.4.refs_0_.refs_1_, bf16[1568,512]{1,0:T(8,128)(2,1)S(1)} %normalize.5.refs_1_.refs_2_, bf16[1568,256]{1,0:T(8,128)(2,1)S(1)} %normalize.6.refs_2_, bf16[1568,128]{1,0:T(8,128)(2,1)S(1)} %normalize.7.refs_3_.refs_2_), custom_call_target="tpu_custom_call" | custom-call | flops 1006632960 | bytes 3932160 | tf_op jit(solution)/shard_map/select/pallas_call | solution.py:105
  26.1 10.6 %collective-permute-done.2 = bf16[4,32,1536]{2,1,0:T(8,128)(2,1)} collective-permute-done((bf16[4,32,1536]{2,1,0:T(8,128)(2,1)}, bf16[4,32,1536]{2,1,0:T(8,128)(2,1)}, u32[]{:S(2)}, u32[]{:S(2)}) %collective-permute-start.2) | collective-permute-done | bytes 393248 | tf_op jit(solution)/shard_map/ppermute | solution.py:298
  45.4 4.6 %collective-permute-done.3 = bf16[32,1536]{1,0:T(8,128)(2,1)S(1)} collective-permute-done((bf16[32,1536]{1,0:T(8,128)(2,1)}, bf16[32,1536]{1,0:T(8,128)(2,1)S(1)}, u32[]{:S(2)}, u32[]{:S(2)}) %collective-permute-start.3) | collective-permute-done | bytes 98336 | tf_op jit(solution)/shard_map/ppermute | solution.py:298
  64.1 45.5 %collective-permute-done.7.refs_2_ = bf16[1568,128]{1,0:T(8,128)(2,1)S(1)} collective-permute-done((bf16[1568,128]{1,0:T(8,128)(2,1)S(1)}, bf16[1568,128]{1,0:T(8,128)(2,1)S(1)}, u32[]{:S(2)}, u32[]{:S(2)}) %collective-permute-start.7) | collective-permute-done | bytes 401440 | tf_op jit(solution)/shard_map/ppermute | solution.py:298
  112.9 5.7 %correlate.18 = (f32[1,32,32,10240]{3,2,1,0:T(8,128)}, bf16[32,32,512]{2,1,0:T(8,128)(2,1)S(1)}) custom-call(s32[1]{0:T(128)} %bitcast.me_ref, bf16[1024,1664]{1,0:T(8,128)(2,1)S(1)} %hankel.2.refs_0_, bf16[1024,1664]{1,0:T(8,128)(2,1)S(1)} %hankel.3.refs_1_, bf16[1568,512]{1,0:T(8,128)(2,1)S(1)} %normalize.5.refs_1_.refs_2_, ...), custom_call_target="tpu_custom_call", output_to_operand_aliasing={{0}: (4, {})} | custom-call | flops 3489660928 | bytes 3702784 | tf_op jit(solution)/shard_map/correlate/pallas_call | solution.py:245
  118.6 3.5 correlate.19
  122.1 3.3 correlate.20
  126.0 17.3 %collective-permute-done.23.got_ref = bf16[32,32,128]{2,1,0:T(8,128)(2,1)S(1)} collective-permute-done((bf16[32,32,128]{2,1,0:T(8,128)(2,1)S(1)}, bf16[32,32,128]{2,1,0:T(8,128)(2,1)S(1)}, u32[]{:S(2)}, u32[]{:S(2)}) %collective-permute-start.23) | collective-permute-done | bytes 262176 | tf_op jit(solution)/shard_map/ppermute | solution.py:298
  145.5 4.0 %collective-permute-start.19 = (bf16[1568,512]{1,0:T(8,128)(2,1)}, bf16[1568,512]{1,0:T(8,128)(2,1)}, u32[]{:S(2)}, u32[]{:S(2)}) collective-permute-start(bf16[1568,512]{1,0:T(8,128)(2,1)} %collective-permute-done.18.refs_3_), channel_id=1, source_target_pairs={{2,0},{3,1},{4,6},{5,7},{10,8},{11,9},{12,14},{13,15},{18,16},{19,... | collective-permute-start | bytes 4816904 | tf_op jit(solution)/shard_map/ppermute | solution.py:298
  158.0 5.4 %correlate.22 = (f32[1,32,32,10240]{3,2,1,0:T(8,128)}, bf16[32,32,384]{2,1,0:T(8,128)(2,1)S(1)}) custom-call(s32[1]{0:T(128)} %bitcast.me_ref, bf16[1024,1664]{1,0:T(8,128)(2,1)S(1)} %hankel.2.refs_0_, bf16[1024,1664]{1,0:T(8,128)(2,1)S(1)} %hankel.3.refs_1_, bf16[1568,384]{1,0:T(8,128)(2,1)S(1)} %collective-permute-done.20.refs_2_, ...), custom_call_target="tpu_custom_call", output_to_operand_aliasing={{0}: (4, {})} | custom-call | flops 2617245696 | bytes 2777088 | tf_op jit(solution)/shard_map/correlate/pallas_call | solution.py:245
  163.5 23.8 %collective-permute-done.24.got_ref = bf16[32,32,256]{2,1,0:T(8,128)(2,1)S(1)} collective-permute-done((bf16[32,32,256]{2,1,0:T(8,128)(2,1)S(1)}, bf16[32,32,256]{2,1,0:T(8,128)(2,1)S(1)}, u32[]{:S(2)}, u32[]{:S(2)}) %collective-permute-start.24) | collective-permute-done | bytes 524320 | tf_op jit(solution)/shard_map/ppermute | solution.py:298
  191.4 7.1 %correlate.23 = (f32[1,32,32,10240]{3,2,1,0:T(8,128)}, bf16[32,32,512]{2,1,0:T(8,128)(2,1)S(1)}) custom-call(s32[1]{0:T(128)} %bitcast.me_ref, bf16[1024,1664]{1,0:T(8,128)(2,1)S(1)} %hankel.2.refs_0_, bf16[1024,1664]{1,0:T(8,128)(2,1)S(1)} %hankel.3.refs_1_, bf16[1568,512]{1,0:T(8,128)(2,1)} %collective-permute-done.13.refs_2_, ...), custom_call_target="tpu_custom_call", output_to_operand_aliasing={{0}: (4, {})} | custom-call | flops 3489660928 | bytes 3702784 | tf_op jit(solution)/shard_map/correlate/pallas_call | solution.py:245
  198.8 3.5 correlate.24
  202.3 5.4 %collective-permute-done.22.got_ref = bf16[32,32,384]{2,1,0:T(8,128)(2,1)S(1)} collective-permute-done((bf16[32,32,384]{2,1,0:T(8,128)(2,1)S(1)}, bf16[32,32,384]{2,1,0:T(8,128)(2,1)S(1)}, u32[]{:S(2)}, u32[]{:S(2)}) %collective-permute-start.22) | collective-permute-done | bytes 786464 | tf_op jit(solution)/shard_map/ppermute | solution.py:298
  209.4 3.3 correlate.25
  219.9 7.6 %correlate.26 = (f32[1,32,32,10240]{3,2,1,0:T(8,128)}, bf16[32,32,512]{2,1,0:T(8,128)(2,1)S(1)}) custom-call(s32[1]{0:T(128)} %bitcast.me_ref, bf16[1024,1664]{1,0:T(8,128)(2,1)S(1)} %hankel.2.refs_0_, bf16[1024,1664]{1,0:T(8,128)(2,1)S(1)} %hankel.3.refs_1_, bf16[1568,512]{1,0:T(8,128)(2,1)} %collective-permute-done.19.refs_2_, ...), custom_call_target="tpu_custom_call", output_to_operand_aliasing={{0}: (5, {})} | custom-call | flops 3489660928 | bytes 3702784 | tf_op jit(solution)/shard_map/correlate/pallas_call | solution.py:245
  227.5 16.8 %collective-permute-done.31.got_ref = bf16[32,32,128]{2,1,0:T(8,128)(2,1)S(1)} collective-permute-done((bf16[32,32,128]{2,1,0:T(8,128)(2,1)S(1)}, bf16[32,32,128]{2,1,0:T(8,128)(2,1)S(1)}, u32[]{:S(2)}, u32[]{:S(2)}) %collective-permute-start.31) | collective-permute-done | bytes 262176 | tf_op jit(solution)/shard_map/ppermute | solution.py:298
  250.0 3.3 collective-permute-start.16
  256.5 7.1 %correlate.27 = (f32[1,32,32,10240]{3,2,1,0:T(8,128)}, bf16[32,32,384]{2,1,0:T(8,128)(2,1)S(1)}) custom-call(s32[1]{0:T(128)} %bitcast.me_ref, bf16[1024,1664]{1,0:T(8,128)(2,1)S(1)} %hankel.2.refs_0_, bf16[1024,1664]{1,0:T(8,128)(2,1)S(1)} %hankel.3.refs_1_, bf16[1568,384]{1,0:T(8,128)(2,1)} %collective-permute-done.30.refs_2_, ...), custom_call_target="tpu_custom_call", output_to_operand_aliasing={{0}: (5, {})} | custom-call | flops 2617245696 | bytes 2777088 | tf_op jit(solution)/shard_map/correlate/pallas_call | solution.py:245
  263.6 17.6 %collective-permute-done.16.refs_3_ = bf16[1568,128]{1,0:T(8,128)(2,1)S(1)} collective-permute-done((bf16[1568,128]{1,0:T(8,128)(2,1)S(1)}, bf16[1568,128]{1,0:T(8,128)(2,1)S(1)}, u32[]{:S(2)}, u32[]{:S(2)}) %collective-permute-start.16) | collective-permute-done | bytes 401440 | tf_op jit(solution)/shard_map/ppermute | solution.py:298
  283.0 3.6 correlate.28
  289.7 3.3 correlate.29
  296.1 5.5 %collective-permute-done.36.got_ref = bf16[32,32,384]{2,1,0:T(8,128)(2,1)S(1)} collective-permute-done((bf16[32,32,384]{2,1,0:T(8,128)(2,1)S(1)}, bf16[32,32,384]{2,1,0:T(8,128)(2,1)S(1)}, u32[]{:S(2)}, u32[]{:S(2)}) %collective-permute-start.36) | collective-permute-done | bytes 786464 | tf_op jit(solution)/shard_map/ppermute | solution.py:298
  304.2 4.5 %collective-permute-done.35.got_ref = bf16[32,32,256]{2,1,0:T(8,128)(2,1)S(1)} collective-permute-done((bf16[32,32,256]{2,1,0:T(8,128)(2,1)S(1)}, bf16[32,32,256]{2,1,0:T(8,128)(2,1)S(1)}, u32[]{:S(2)}, u32[]{:S(2)}) %collective-permute-start.35) | collective-permute-done | bytes 524320 | tf_op jit(solution)/shard_map/ppermute | solution.py:298
  312.3 7.6 %correlate.30 = (f32[1,32,32,10240]{3,2,1,0:T(8,128)}, bf16[32,32,512]{2,1,0:T(8,128)(2,1)S(1)}) custom-call(s32[1]{0:T(128)} %bitcast.me_ref, bf16[1024,1664]{1,0:T(8,128)(2,1)S(1)} %hankel.2.refs_0_, bf16[1024,1664]{1,0:T(8,128)(2,1)S(1)} %hankel.3.refs_1_, bf16[1568,512]{1,0:T(8,128)(2,1)} %collective-permute-done.15.refs_2_, ...), custom_call_target="tpu_custom_call", output_to_operand_aliasing={{0}: (5, {})} | custom-call | flops 3489660928 | bytes 3702784 | tf_op jit(solution)/shard_map/correlate/pallas_call | solution.py:245
  324.2 5.5 %correlate.31 = (f32[1,32,32,10240]{3,2,1,0:T(8,128)}, bf16[32,32,384]{2,1,0:T(8,128)(2,1)S(1)}) custom-call(s32[1]{0:T(128)} %bitcast.me_ref, bf16[1024,1664]{1,0:T(8,128)(2,1)S(1)} %hankel.2.refs_0_, bf16[1024,1664]{1,0:T(8,128)(2,1)S(1)} %hankel.3.refs_1_, bf16[1568,384]{1,0:T(8,128)(2,1)S(1)} %collective-permute-done.39.refs_2_, ...), custom_call_target="tpu_custom_call", output_to_operand_aliasing={{0}: (5, {})} | custom-call | flops 2617245696 | bytes 2777088 | tf_op jit(solution)/shard_map/correlate/pallas_call | solution.py:245
  332.7 13.3 %collective-permute-done.37.got_ref = bf16[32,32,512]{2,1,0:T(8,128)(2,1)S(1)} collective-permute-done((bf16[32,32,512]{2,1,0:T(8,128)(2,1)S(1)}, bf16[32,32,512]{2,1,0:T(8,128)(2,1)S(1)}, u32[]{:S(2)}, u32[]{:S(2)}) %collective-permute-start.37) | collective-permute-done | bytes 1048608 | tf_op jit(solution)/shard_map/ppermute | solution.py:298
  347.4 3.6 correlate.32
  351.3 3.3 correlate.33
  356.3 6.5 %collective-permute-done.42.got_ref = bf16[32,32,384]{2,1,0:T(8,128)(2,1)S(1)} collective-permute-done((bf16[32,32,384]{2,1,0:T(8,128)(2,1)S(1)}, bf16[32,32,384]{2,1,0:T(8,128)(2,1)S(1)}, u32[]{:S(2)}, u32[]{:S(2)}) %collective-permute-start.42) | collective-permute-done | bytes 786464 | tf_op jit(solution)/shard_map/ppermute | solution.py:298
  364.0 5.1 %collective-permute-done.41.got_ref = bf16[32,32,256]{2,1,0:T(8,128)(2,1)S(1)} collective-permute-done((bf16[32,32,256]{2,1,0:T(8,128)(2,1)S(1)}, bf16[32,32,256]{2,1,0:T(8,128)(2,1)S(1)}, u32[]{:S(2)}, u32[]{:S(2)}) %collective-permute-start.41) | collective-permute-done | bytes 524320 | tf_op jit(solution)/shard_map/ppermute | solution.py:298
  (125 shorter events, 106.9 us)
Async XLA Ops:
  43.4 106.1 %collective-permute-start.13 = (bf16[1568,512]{1,0:T(8,128)(2,1)S(1)}, bf16[1568,512]{1,0:T(8,128)(2,1)}, u32[]{:S(2)}, u32[]{:S(2)}) collective-permute-start(bf16[1568,512]{1,0:T(8,128)(2,1)S(1)} %normalize.5.refs_1_.refs_2_), channel_id=1, source_target_pairs={{0,2},{1,3},{2,0},{3,1},{4,6},{5,7},{6,4},{7,5},{8,10},{9,11},{10,... | collective-permute-start | bytes 4816904 | tf_op jit(solution)/shard_map/ppermute | solution.py:298
  44.3 66.9 %collective-permute-start.10 = (bf16[1568,256]{1,0:T(8,128)(2,1)}, bf16[1568,256]{1,0:T(8,128)(2,1)S(1)}, u32[]{:S(2)}, u32[]{:S(2)}) collective-permute-start(bf16[1568,256]{1,0:T(8,128)(2,1)} %copy-done.1), channel_id=1, source_target_pairs={{0,2},{1,3},{2,0},{3,1},{4,6},{5,7},{6,4},{7,5},{8,10},{9,11},{10,... | collective-permute-start | bytes 2408456 | tf_op jit(solution)/shard_map/ppermute | solution.py:298
  50.1 59.6 %collective-permute-start.7 = (bf16[1568,128]{1,0:T(8,128)(2,1)S(1)}, bf16[1568,128]{1,0:T(8,128)(2,1)S(1)}, u32[]{:S(2)}, u32[]{:S(2)}) collective-permute-start(bf16[1568,128]{1,0:T(8,128)(2,1)S(1)} %normalize.7.refs_3_.refs_2_), channel_id=1, source_target_pairs={{0,2},{1,3},{2,0},{3,1},{4,6},{5,7},{6,4},{7,5},{8,10},{9,11},{10,... | collective-permute-start | bytes 1204232 | tf_op jit(solution)/shard_map/ppermute | solution.py:298
  50.1 95.4 %collective-permute-start.18 = (bf16[1568,512]{1,0:T(8,128)(2,1)S(1)}, bf16[1568,512]{1,0:T(8,128)(2,1)}, u32[]{:S(2)}, u32[]{:S(2)}) collective-permute-start(bf16[1568,512]{1,0:T(8,128)(2,1)S(1)} %normalize.5.refs_1_.refs_2_), channel_id=1, source_target_pairs={{2,4},{3,5},{4,2},{5,3},{10,12},{11,13},{12,10},{13,11},{18,20},{1... | collective-permute-start | bytes 4816904 | tf_op jit(solution)/shard_map/ppermute | solution.py:298
  60.2 65.2 %collective-permute-start.27 = (bf16[1568,256]{1,0:T(8,128)(2,1)S(1)}, bf16[1568,256]{1,0:T(8,128)(2,1)S(1)}, u32[]{:S(2)}, u32[]{:S(2)}) collective-permute-start(bf16[1568,256]{1,0:T(8,128)(2,1)S(1)} %copy-done.2), channel_id=1, source_target_pairs={{2,4},{3,5},{4,2},{5,3},{10,12},{11,13},{12,10},{13,11},{18,20},{1... | collective-permute-start | bytes 2408456 | tf_op jit(solution)/shard_map/ppermute | solution.py:298
  109.7 43.1 %collective-permute-start.21 = (bf16[1568,384]{1,0:T(8,128)(2,1)S(1)}, bf16[1568,384]{1,0:T(8,128)(2,1)S(1)}, u32[]{:S(2)}, u32[]{:S(2)}) collective-permute-start(bf16[1568,384]{1,0:T(8,128)(2,1)S(1)} %normalize.4.refs_0_.refs_1_), channel_id=1, source_target_pairs={{0,1},{1,0},{2,3},{3,2},{4,5},{5,4},{6,7},{7,6},{8,9},{9,8},{10,11... | collective-permute-start | bytes 3612680 | tf_op jit(solution)/shard_map/ppermute | solution.py:298
  111.2 43.4 %collective-permute-start.20 = (bf16[1568,384]{1,0:T(8,128)(2,1)S(1)}, bf16[1568,384]{1,0:T(8,128)(2,1)S(1)}, u32[]{:S(2)}, u32[]{:S(2)}) collective-permute-start(bf16[1568,384]{1,0:T(8,128)(2,1)S(1)} %normalize.4.refs_0_.refs_1_), channel_id=1, source_target_pairs={{0,2},{1,3},{2,0},{3,1},{4,6},{5,7},{6,4},{7,5},{8,10},{9,11},{10,... | collective-permute-start | bytes 3612680 | tf_op jit(solution)/shard_map/ppermute | solution.py:298
  143.2 45.8 %collective-permute-start.29 = (bf16[1568,384]{1,0:T(8,128)(2,1)S(1)}, bf16[1568,384]{1,0:T(8,128)(2,1)}, u32[]{:S(2)}, u32[]{:S(2)}) collective-permute-start(bf16[1568,384]{1,0:T(8,128)(2,1)S(1)} %normalize.4.refs_0_.refs_1_), channel_id=1, source_target_pairs={{2,4},{3,5},{4,2},{5,3},{10,12},{11,13},{12,10},{13,11},{18,20},{1... | collective-permute-start | bytes 3612680 | tf_op jit(solution)/shard_map/ppermute | solution.py:298
  145.5 71.7 %collective-permute-start.19 = (bf16[1568,512]{1,0:T(8,128)(2,1)}, bf16[1568,512]{1,0:T(8,128)(2,1)}, u32[]{:S(2)}, u32[]{:S(2)}) collective-permute-start(bf16[1568,512]{1,0:T(8,128)(2,1)} %collective-permute-done.18.refs_3_), channel_id=1, source_target_pairs={{2,0},{3,1},{4,6},{5,7},{10,8},{11,9},{12,14},{13,15},{18,16},{19,... | collective-permute-start | bytes 4816904 | tf_op jit(solution)/shard_map/ppermute | solution.py:298
  149.5 68.0 %collective-permute-start.14 = (bf16[1568,512]{1,0:T(8,128)(2,1)}, bf16[1568,512]{1,0:T(8,128)(2,1)}, u32[]{:S(2)}, u32[]{:S(2)}) collective-permute-start(bf16[1568,512]{1,0:T(8,128)(2,1)} %collective-permute-done.13.refs_2_), channel_id=1, source_target_pairs={{2,4},{3,5},{4,2},{5,3},{10,12},{11,13},{12,10},{13,11},{18,20},{1... | collective-permute-start | bytes 4816904 | tf_op jit(solution)/shard_map/ppermute | solution.py:298
  152.8 45.7 %collective-permute-start.25 = (bf16[32,32,512]{2,1,0:T(8,128)(2,1)S(1)}, bf16[32,32,512]{2,1,0:T(8,128)(2,1)S(1)}, u32[]{:S(2)}, u32[]{:S(2)}) collective-permute-start(bf16[32,32,512]{2,1,0:T(8,128)(2,1)S(1)} %get-tuple-element.41), channel_id=1, source_target_pairs={{0,1},{1,0},{2,3},{3,2},{4,5},{5,4},{6,7},{7,6},{8,9},{9,8},{10,11... | collective-permute-start | bytes 3145736 | tf_op jit(solution)/shard_map/ppermute | solution.py:298
  154.6 32.7 %collective-permute-start.24 = (bf16[32,32,256]{2,1,0:T(8,128)(2,1)S(1)}, bf16[32,32,256]{2,1,0:T(8,128)(2,1)S(1)}, u32[]{:S(2)}, u32[]{:S(2)}) collective-permute-start(bf16[32,32,256]{2,1,0:T(8,128)(2,1)S(1)} %get-tuple-element.40), channel_id=1, source_target_pairs={{0,1},{1,0},{2,3},{3,2},{4,5},{5,4},{6,7},{7,6},{8,9},{9,8},{10,11... | collective-permute-start | bytes 1572872 | tf_op jit(solution)/shard_map/ppermute | solution.py:298
  187.3 20.4 %collective-permute-start.22 = (bf16[32,32,384]{2,1,0:T(8,128)(2,1)S(1)}, bf16[32,32,384]{2,1,0:T(8,128)(2,1)S(1)}, u32[]{:S(2)}, u32[]{:S(2)}) collective-permute-start(bf16[32,32,384]{2,1,0:T(8,128)(2,1)S(1)} %get-tuple-element.38), channel_id=1, source_target_pairs={{0,1},{1,0},{2,3},{3,2},{4,5},{5,4},{6,7},{7,6},{8,9},{9,8},{10,11... | collective-permute-start | bytes 2359304 | tf_op jit(solution)/shard_map/ppermute | solution.py:298
  189.0 58.4 %collective-permute-start.30 = (bf16[1568,384]{1,0:T(8,128)(2,1)}, bf16[1568,384]{1,0:T(8,128)(2,1)}, u32[]{:S(2)}, u32[]{:S(2)}) collective-permute-start(bf16[1568,384]{1,0:T(8,128)(2,1)} %collective-permute-done.29.refs_3_), channel_id=1, source_target_pairs={{2,0},{3,1},{4,6},{5,7},{10,8},{11,9},{12,14},{13,15},{18,16},{19,... | collective-permute-start | bytes 3612680 | tf_op jit(solution)/shard_map/ppermute | solution.py:298
  198.5 51.5 %collective-permute-start.33 = (bf16[32,32,512]{2,1,0:T(8,128)(2,1)S(1)}, bf16[32,32,512]{2,1,0:T(8,128)(2,1)S(1)}, u32[]{:S(2)}, u32[]{:S(2)}) collective-permute-start(bf16[32,32,512]{2,1,0:T(8,128)(2,1)S(1)} %get-tuple-element.49), channel_id=1, source_target_pairs={{0,1},{1,0},{2,3},{3,2},{4,5},{5,4},{6,7},{7,6},{8,9},{9,8},{10,11... | collective-permute-start | bytes 3145736 | tf_op jit(solution)/shard_map/ppermute | solution.py:298
  207.7 38.4 %collective-permute-start.32 = (bf16[32,32,256]{2,1,0:T(8,128)(2,1)S(1)}, bf16[32,32,256]{2,1,0:T(8,128)(2,1)S(1)}, u32[]{:S(2)}, u32[]{:S(2)}) collective-permute-start(bf16[32,32,256]{2,1,0:T(8,128)(2,1)S(1)} %get-tuple-element.48), channel_id=1, source_target_pairs={{0,1},{1,0},{2,3},{3,2},{4,5},{5,4},{6,7},{7,6},{8,9},{9,8},{10,11... | collective-permute-start | bytes 1572872 | tf_op jit(solution)/shard_map/ppermute | solution.py:298
  217.2 27.2 %collective-permute-start.31 = (bf16[32,32,128]{2,1,0:T(8,128)(2,1)S(1)}, bf16[32,32,128]{2,1,0:T(8,128)(2,1)S(1)}, u32[]{:S(2)}, u32[]{:S(2)}) collective-permute-start(bf16[32,32,128]{2,1,0:T(8,128)(2,1)S(1)} %get-tuple-element.47), channel_id=1, source_target_pairs={{0,1},{1,0},{2,3},{3,2},{4,5},{5,4},{6,7},{7,6},{8,9},{9,8},{10,11... | collective-permute-start | bytes 786440 | tf_op jit(solution)/shard_map/ppermute | solution.py:298
  217.5 94.9 %collective-permute-start.15 = (bf16[1568,512]{1,0:T(8,128)(2,1)}, bf16[1568,512]{1,0:T(8,128)(2,1)}, u32[]{:S(2)}, u32[]{:S(2)}) collective-permute-start(bf16[1568,512]{1,0:T(8,128)(2,1)} %collective-permute-done.14.refs_3_), channel_id=1, source_target_pairs={{2,0},{3,1},{4,6},{5,7},{10,8},{11,9},{12,14},{13,15},{18,16},{19,... | collective-permute-start | bytes 4816904 | tf_op jit(solution)/shard_map/ppermute | solution.py:298
  244.3 42.3 %collective-permute-start.26 = (bf16[32,32,512]{2,1,0:T(8,128)(2,1)S(1)}, bf16[32,32,512]{2,1,0:T(8,128)(2,1)S(1)}, u32[]{:S(2)}, u32[]{:S(2)}) collective-permute-start(bf16[32,32,512]{2,1,0:T(8,128)(2,1)S(1)} %get-tuple-element.46), channel_id=1, source_target_pairs={{0,1},{1,0},{2,3},{3,2},{4,5},{5,4},{6,7},{7,6},{8,9},{9,8},{10,11... | collective-permute-start | bytes 3145736 | tf_op jit(solution)/shard_map/ppermute | solution.py:298
  246.1 35.4 %collective-permute-start.28 = (bf16[1568,256]{1,0:T(8,128)(2,1)S(1)}, bf16[1568,256]{1,0:T(8,128)(2,1)S(1)}, u32[]{:S(2)}, u32[]{:S(2)}) collective-permute-start(bf16[1568,256]{1,0:T(8,128)(2,1)S(1)} %copy-done.6), channel_id=1, source_target_pairs={{2,0},{3,1},{4,6},{5,7},{10,8},{11,9},{12,14},{13,15},{18,16},{19,... | collective-permute-start | bytes 2408456 | tf_op jit(solution)/shard_map/ppermute | solution.py:298
  247.4 46.0 %collective-permute-start.38 = (bf16[1568,384]{1,0:T(8,128)(2,1)S(1)}, bf16[1568,384]{1,0:T(8,128)(2,1)S(1)}, u32[]{:S(2)}, u32[]{:S(2)}) collective-permute-start(bf16[1568,384]{1,0:T(8,128)(2,1)S(1)} %collective-permute-done.20.refs_2_), channel_id=1, source_target_pairs={{2,4},{3,5},{4,2},{5,3},{10,12},{11,13},{12,10},{13,11},{18,20},{1... | collective-permute-start | bytes 3612680 | tf_op jit(solution)/shard_map/ppermute | solution.py:298
  250.0 31.2 %collective-permute-start.16 = (bf16[1568,128]{1,0:T(8,128)(2,1)S(1)}, bf16[1568,128]{1,0:T(8,128)(2,1)S(1)}, u32[]{:S(2)}, u32[]{:S(2)}) collective-permute-start(bf16[1568,128]{1,0:T(8,128)(2,1)S(1)} %normalize.7.refs_3_.refs_2_), channel_id=1, source_target_pairs={{2,4},{3,5},{4,2},{5,3},{10,12},{11,13},{12,10},{13,11},{18,20},{1... | collective-permute-start | bytes 1204232 | tf_op jit(solution)/shard_map/ppermute | solution.py:298
  281.2 20.4 %collective-permute-start.36 = (bf16[32,32,384]{2,1,0:T(8,128)(2,1)S(1)}, bf16[32,32,384]{2,1,0:T(8,128)(2,1)S(1)}, u32[]{:S(2)}, u32[]{:S(2)}) collective-permute-start(bf16[32,32,384]{2,1,0:T(8,128)(2,1)S(1)} %get-tuple-element.55), channel_id=1, source_target_pairs={{0,1},{1,0},{2,3},{3,2},{4,5},{5,4},{6,7},{7,6},{8,9},{9,8},{10,11... | collective-permute-start | bytes 2359304 | tf_op jit(solution)/shard_map/ppermute | solution.py:298
  286.6 22.1 %collective-permute-start.35 = (bf16[32,32,256]{2,1,0:T(8,128)(2,1)S(1)}, bf16[32,32,256]{2,1,0:T(8,128)(2,1)S(1)}, u32[]{:S(2)}, u32[]{:S(2)}) collective-permute-start(bf16[32,32,256]{2,1,0:T(8,128)(2,1)S(1)} %get-tuple-element.54), channel_id=1, source_target_pairs={{0,1},{1,0},{2,3},{3,2},{4,5},{5,4},{6,7},{7,6},{8,9},{9,8},{10,11... | collective-permute-start | bytes 1572872 | tf_op jit(solution)/shard_map/ppermute | solution.py:298
  293.1 18.4 %collective-permute-start.34 = (bf16[32,32,128]{2,1,0:T(8,128)(2,1)S(1)}, bf16[32,32,128]{2,1,0:T(8,128)(2,1)S(1)}, u32[]{:S(2)}, u32[]{:S(2)}) collective-permute-start(bf16[32,32,128]{2,1,0:T(8,128)(2,1)S(1)} %get-tuple-element.53), channel_id=1, source_target_pairs={{0,1},{1,0},{2,3},{3,2},{4,5},{5,4},{6,7},{7,6},{8,9},{9,8},{10,11... | collective-permute-start | bytes 786440 | tf_op jit(solution)/shard_map/ppermute | solution.py:298
  293.4 26.9 %collective-permute-start.11 = (bf16[1568,256]{1,0:T(8,128)(2,1)S(1)}, bf16[1568,256]{1,0:T(8,128)(2,1)S(1)}, u32[]{:S(2)}, u32[]{:S(2)}) collective-permute-start(bf16[1568,256]{1,0:T(8,128)(2,1)S(1)} %copy-done.4), channel_id=1, source_target_pairs={{2,4},{3,5},{4,2},{5,3},{10,12},{11,13},{12,10},{13,11},{18,20},{1... | collective-permute-start | bytes 2408456 | tf_op jit(solution)/shard_map/ppermute | solution.py:298
  301.6 22.6 %collective-permute-start.39 = (bf16[1568,384]{1,0:T(8,128)(2,1)S(1)}, bf16[1568,384]{1,0:T(8,128)(2,1)S(1)}, u32[]{:S(2)}, u32[]{:S(2)}) collective-permute-start(bf16[1568,384]{1,0:T(8,128)(2,1)S(1)} %collective-permute-done.38.refs_3_), channel_id=1, source_target_pairs={{2,0},{3,1},{4,6},{5,7},{10,8},{11,9},{12,14},{13,15},{18,16},{19,... | collective-permute-start | bytes 3612680 | tf_op jit(solution)/shard_map/ppermute | solution.py:298
  320.0 26.0 %collective-permute-start.37 = (bf16[32,32,512]{2,1,0:T(8,128)(2,1)S(1)}, bf16[32,32,512]{2,1,0:T(8,128)(2,1)S(1)}, u32[]{:S(2)}, u32[]{:S(2)}) collective-permute-start(bf16[32,32,512]{2,1,0:T(8,128)(2,1)S(1)} %get-tuple-element.57), channel_id=1, source_target_pairs={{0,1},{1,0},{2,3},{3,2},{4,5},{5,4},{6,7},{7,6},{8,9},{9,8},{10,11... | collective-permute-start | bytes 3145736 | tf_op jit(solution)/shard_map/ppermute | solution.py:298
  320.3 27.1 %collective-permute-start.12 = (bf16[1568,256]{1,0:T(8,128)(2,1)S(1)}, bf16[1568,256]{1,0:T(8,128)(2,1)S(1)}, u32[]{:S(2)}, u32[]{:S(2)}) collective-permute-start(bf16[1568,256]{1,0:T(8,128)(2,1)S(1)} %collective-permute-done.11.refs_3_), channel_id=1, source_target_pairs={{2,0},{3,1},{4,6},{5,7},{10,8},{11,9},{12,14},{13,15},{18,16},{19,... | collective-permute-start | bytes 2408456 | tf_op jit(solution)/shard_map/ppermute | solution.py:298
  329.7 33.2 %collective-permute-start.42 = (bf16[32,32,384]{2,1,0:T(8,128)(2,1)S(1)}, bf16[32,32,384]{2,1,0:T(8,128)(2,1)S(1)}, u32[]{:S(2)}, u32[]{:S(2)}) collective-permute-start(bf16[32,32,384]{2,1,0:T(8,128)(2,1)S(1)} %get-tuple-element.63), channel_id=1, source_target_pairs={{0,1},{1,0},{2,3},{3,2},{4,5},{5,4},{6,7},{7,6},{8,9},{9,8},{10,11... | collective-permute-start | bytes 2359304 | tf_op jit(solution)/shard_map/ppermute | solution.py:298
  331.4 19.9 %collective-permute-start.9 = (bf16[1568,128]{1,0:T(8,128)(2,1)S(1)}, bf16[1568,128]{1,0:T(8,128)(2,1)S(1)}, u32[]{:S(2)}, u32[]{:S(2)}) collective-permute-start(bf16[1568,128]{1,0:T(8,128)(2,1)S(1)} %collective-permute-done.8.refs_3_), channel_id=1, source_target_pairs={{2,0},{3,1},{4,6},{5,7},{10,8},{11,9},{12,14},{13,15},{18,16},{19,... | collective-permute-start | bytes 1204232 | tf_op jit(solution)/shard_map/ppermute | solution.py:298
  350.9 18.2 %collective-permute-start.41 = (bf16[32,32,256]{2,1,0:T(8,128)(2,1)S(1)}, bf16[32,32,256]{2,1,0:T(8,128)(2,1)S(1)}, u32[]{:S(2)}, u32[]{:S(2)}) collective-permute-start(bf16[32,32,256]{2,1,0:T(8,128)(2,1)S(1)} %get-tuple-element.62), channel_id=1, source_target_pairs={{0,1},{1,0},{2,3},{3,2},{4,5},{5,4},{6,7},{7,6},{8,9},{9,8},{10,11... | collective-permute-start | bytes 1572872 | tf_op jit(solution)/shard_map/ppermute | solution.py:298
  (21 other events, 397.2 us)
